TPU v7x, 256 devices: a whole 4x4x8 slice. The times are simulated.
256 devices in a mesh: table: 64 (over y, z, core), rep: 4 (over x).
Axes of the slice: x: 4, y: 4, z: 8, core: 2. Of those that a mesh axis runs over, the one named last changes fastest.
Arguments:
- embedding_table: float32 [131072, 128], P('table'), may hold values from -1.8 to 1.8
- row_history: float32 [131072], P('table'), may hold values from 0.5 to 4
- hot_table: float32 [262144, 128], P('table'), may hold values from -1.8 to 1.8
- hot_history: float32 [262144], P('table'), may hold values from 10 to 1000
- hot_owner: int32 [1], replicated, may hold values from 0 to 63
- cold_index: int32 [4, 4096, 256], P('rep', 'table'), may hold values from 0 to 2047
- cold_counts: int32 [4, 4096], P('rep', 'table'), may hold values from 1 to 256, as said below
- cold_bags: int32 [4, 4096, 256], P('rep', 'table'), may hold values from 0 to 255
- hot_index: int32 [4, 131072], P('rep', 'table'), may hold values from 0 to 4095
- hot_bags: int32 [4, 131072], P('rep', 'table'), may hold values from 0 to 255
- pooled_grad: bfloat16 [4, 16384, 128], P('rep', 'table'), may hold values from -6 to 6
Outputs:
- pooled_bags: bfloat16 [4, 16384, 128], P('rep', 'table')
- next_table: float32 [131072, 128], P('table')
- next_history: float32 [131072], P('table')
- next_hot: float32 [262144, 128], P('table')
- next_squares: float32 [262144], P('table')
Inputs may be any that keep to these rules, and one draw needn't show every extreme that they name: `cold_counts`: slots of a request list past its count are padding. In every draw some owner receives 256 live slots from every device of every replica, and some lists are full.
All inputs are finite; a program needn't handle non-finite values.
Results may differ from a plain program's by a relative error of at most 0.0028.
The roundings to bfloat16 on the way count: a program that leaves them out, or rounds other values in their place, can miss the bound.
Values may be sent and summed in bfloat16 or wider, within the bound.
No kernel may reach another device: no remote copies, remote signals or barrier semaphores. Data moves between devices by JAX's collectives and lax.ppermute only.
A program may use at most 64 MiB of HBM per device.

v0:
```python
import math

import jax
import jax.numpy as jnp
from jax import lax
from jax.sharding import PartitionSpec as P

learn_rate = 0.1
epsilon = 1e-08


def from_root(block, axis, source):
    block = jnp.where(lax.axis_index(axis) == source, block, jnp.zeros_like(block))
    return lax.psum(block, axis)


def adagrad_rows(weights, history, gradient):
    updated = history + jnp.mean(gradient * gradient, axis=1)
    return (weights - learn_rate * gradient / (jnp.sqrt(updated)[:, None] + epsilon), updated)


def pool_bags(table_rows, bag_ids, bag_count):
    row_total = table_rows.shape[0]
    row_width = table_rows.shape[1]
    block_size = math.gcd(row_total, 2048)
    row_blocks = table_rows.reshape(row_total // block_size, block_size, row_width)
    bag_blocks = bag_ids.reshape(row_total // block_size, block_size)
    labels = jnp.arange(bag_count, dtype=jnp.int32)

    def add_block(running, pair_item):
        block_rows, block_bags = pair_item
        onehot = (block_bags[None, :] == labels[:, None]).astype(jnp.bfloat16)
        return (running + jnp.dot(onehot, block_rows, preferred_element_type=jnp.float32), None)

    initial = jnp.zeros((bag_count, row_width), jnp.float32)
    pooled, unused = lax.scan(add_block, initial, (row_blocks, bag_blocks))
    return pooled


def spread_bags(bag_grad, bag_ids):
    row_total = bag_ids.shape[0]
    block_size = math.gcd(row_total, 2048)
    bag_blocks = bag_ids.reshape(row_total // block_size, block_size)
    labels = jnp.arange(bag_grad.shape[0], dtype=jnp.int32)

    def one_block(unused_carry, block_bags):
        onehot = (block_bags[None, :] == labels[:, None]).astype(jnp.bfloat16)
        spread = lax.dot_general(
            onehot, bag_grad, (((0,), (0,)), ((), ())), preferred_element_type=jnp.float32
        )
        return (unused_carry, spread.astype(jnp.bfloat16))

    unused, spread = lax.scan(one_block, jnp.zeros((), jnp.int32), bag_blocks)
    return spread.reshape(row_total, bag_grad.shape[1])


def shards(
    embedding_table,
    row_history,
    hot_table,
    hot_history,
    hot_owner,
    cold_index,
    cold_counts,
    cold_bags,
    hot_index,
    hot_bags,
    pooled_grad,
):
    peer_count = lax.axis_size("table")
    index_rows = cold_index[0]
    bag_ids = cold_bags[0]
    slot_counts = cold_counts[0]
    slot_total = index_rows.shape[1]
    bag_count = pooled_grad.shape[1]
    row_width = embedding_table.shape[1]
    row_count = embedding_table.shape[0]
    live_mask = jnp.arange(slot_total, dtype=jnp.int32)[None, :] < slot_counts[:, None]
    masked_bags = jnp.where(live_mask, bag_ids, -1)
    owner_index = hot_owner[0]
    hot_block = from_root(hot_table.astype(jnp.bfloat16), "table", owner_index)
    received_index = lax.all_to_all(index_rows, "table", split_axis=0, concat_axis=0, tiled=True)
    served = jnp.take(embedding_table, received_index, axis=0).astype(jnp.bfloat16)
    pulled = lax.all_to_all(served, "table", split_axis=0, concat_axis=0, tiled=True)
    hot_pulled = jnp.take(hot_block, hot_index[0], axis=0)
    pooled = pool_bags(pulled.reshape(-1, row_width), masked_bags.reshape(-1), bag_count)
    pooled = pooled + pool_bags(hot_pulled, hot_bags[0], bag_count)
    bag_grad = pooled_grad[0]
    hot_terms = spread_bags(bag_grad, hot_bags[0])
    hot_dense = jax.ops.segment_sum(
        hot_terms.astype(jnp.float32), hot_index[0], num_segments=hot_table.shape[0]
    )
    slot_grad = spread_bags(bag_grad, masked_bags.reshape(-1)).reshape(
        peer_count, slot_total, row_width
    )
    returned = lax.all_to_all(slot_grad, "table", split_axis=0, concat_axis=0, tiled=True)
    dense_grad = jax.ops.segment_sum(
        returned.reshape(-1, row_width).astype(jnp.float32),
        received_index.reshape(-1),
        num_segments=row_count,
    )
    dense_grad = lax.psum(dense_grad.astype(jnp.bfloat16), "rep").astype(jnp.float32)
    next_table, next_history = adagrad_rows(embedding_table, row_history, dense_grad)
    hot_total = lax.psum(hot_dense, ("table", "rep"))
    hot_updated, history_updated = adagrad_rows(hot_table, hot_history, hot_total)
    is_owner = lax.axis_index("table") == owner_index
    next_hot = jnp.where(is_owner, hot_updated, hot_table)
    next_squares = jnp.where(is_owner, history_updated, hot_history)
    return (pooled.astype(jnp.bfloat16)[None], next_table, next_history, next_hot, next_squares)


def solution(mesh):
    in_specs = (
        P("table", None),
        P("table"),
        P("table", None),
        P("table"),
        P(),
        P("rep", "table", None),
        P("rep", "table"),
        P("rep", "table", None),
        P("rep", "table"),
        P("rep", "table"),
        P("rep", "table", None),
    )
    out_specs = (
        P("rep", "table", None),
        P("table", None),
        P("table"),
        P("table", None),
        P("table"),
    )
    return jax.shard_map(shards, mesh=mesh, in_specs=in_specs, out_specs=out_specs, check_vma=False)
```

profile of v0, /device:TPU:128, one launch (start us, length us, event | category | flops | bytes accessed | tf_op | source)
XLA Modules:
  0.0 784.3 jit_solution(6435506943395076284)
XLA Ops:
  9.5 10.4 %all-to-all-start = ((s32[64,1,256]{2,1,0:T(1,128)}), s32[64,1,256]{2,1,0:T(1,128)S(1)}, u32[]{:S(2)}, u32[]{:S(2)}) async-start(s32[64,1,256]{2,1,0:T(1,128)} %all_to_all.16), calls=%async_computation | async-start | bytes 131072 | tf_op jit(solution)/shard_map/all_to_all | solution.py:82
  22.9 19.2 %while.6 = (s32[]{:T(128)}, bf16[8,2048,128]{2,1,0:T(8,128)(2,1)}, s32[8,2048]{1,0:T(8,128)S(1)}, bf16[256,128]{1,0:T(8,128)(2,1)}, s32[]{:T(128)}) while((s32[]{:T(128)}, bf16[8,2048,128]{2,1,0:T(8,128)(2,1)}, s32[8,2048]{1,0:T(8,128)S(1)}, bf16[256,128]{1,0:T(8,128)(2,1)}, s32[]{:T(128)}) %tuple.61), condition=%wide.region_4.5_spmd.clone, body=%wide.region_3.4_spmd.clone.sunk | while | flops 135004160 | bytes 614477 | solution.py:53
  22.9 2.4 fusion.40
  25.4 2.4 fusion.40
  27.8 2.4 fusion.40
  30.2 2.4 fusion.40
  32.6 2.4 fusion.40
  35.0 2.4 fusion.40
  37.4 2.4 fusion.40
  39.7 2.4 fusion.40
  42.1 10.6 %all-to-all-start.2 = ((bf16[64,256,128]{2,1,0:T(8,128)(2,1)}), bf16[64,256,128]{2,1,0:T(8,128)(2,1)}, u32[]{:S(2)}, u32[]{:S(2)}) async-start(bf16[64,256,128]{2,1,0:T(8,128)(2,1)} %bitcast.50), calls=%async_computation.2 | async-start | bytes 8388608 | tf_op jit(solution)/shard_map/all_to_all | solution.py:96
  52.9 55.4 %gather_fusion = bf16[16384,128]{1,0:T(8,128)(2,1)} fusion(f32[2048,128]{1,0:T(8,128)S(1)} %copy-done, s32[16384]{0:T(1024)S(1)} %broadcast_clamp_fusion), kind=kCustom, calls=%fused_computation | custom fusion | bytes 8454144 | tf_op jit(solution)/shard_map/jit(_take)/gather | solution.py:83
  108.3 7.6 select_convert_fusion
  115.9 30.3 %all-to-all-done.2 = bf16[64,256,128]{2,1,0:T(8,128)(2,1)} async-done(((bf16[64,256,128]{2,1,0:T(8,128)(2,1)}), bf16[64,256,128]{2,1,0:T(8,128)(2,1)}, u32[]{:S(2)}, u32[]{:S(2)}) %all-to-all-start.2) | async-done | bytes 4194336 | tf_op jit(solution)/shard_map/all_to_all | solution.py:96
  146.2 8.4 %all-to-all-start.1 = ((bf16[64,256,128]{2,1,0:T(8,128)(2,1)}), bf16[64,256,128]{2,1,0:T(8,128)(2,1)}, u32[]{:S(2)}, u32[]{:S(2)}) async-start(bf16[64,256,128]{2,1,0:T(8,128)(2,1)} %select_convert_fusion), calls=%async_computation.1 | async-start | bytes 8388608 | tf_op jit(solution)/shard_map/all_to_all | solution.py:84
  158.2 13.2 %scatter_custom_fusion.1 = f32[4096,128]{1,0:T(8,128)} fusion(s32[2048]{0:T(1024)S(1)} %bitcast.59, f32[2048,128]{1,0:T(8,128)} %fusion.15, f32[]{:T(128)} %constant.52.clone.1), kind=kCustom, calls=%fused_computation.37 | custom fusion | flops 262144 | bytes 2097664 | tf_op jit(solution)/shard_map/scatter-add | solution.py:90
  171.6 189.8 %all-reduce.4.cloned.1.call-done = bf16[4096,128]{1,0:T(8,128)(2,1)} async-done(((bf16[4096,128]{1,0:T(8,128)(2,1)}), bf16[4096,128]{1,0:T(8,128)(2,1)}) %all-reduce.4.cloned.1.call-update) | async-done | bytes 1048592 | tf_op jit(solution)/shard_map/psum | solution.py:14
  361.4 9.1 %gather_fusion.1 = bf16[2048,128]{1,0:T(8,128)(2,1)} fusion(bf16[4096,128]{1,0:T(8,128)(2,1)} %all-reduce.4.cloned.1.call-done, s32[2048]{0:T(1024)S(1)} %broadcast_clamp_fusion.1), kind=kCustom, calls=%fused_computation.1 | custom fusion | bytes 1056768 | tf_op jit(solution)/shard_map/jit(_take)/gather | solution.py:85
  370.5 259.2 %all-reduce.8.cloned.1.call-done = f32[4096,128]{1,0:T(8,128)} async-done(((f32[4096,128]{1,0:T(8,128)}), f32[4096,128]{1,0:T(8,128)}) %all-reduce.8.cloned.1.call-update) | async-done | bytes 2097168 | tf_op jit(solution)/shard_map/psum | solution.py:104
  629.7 2.4 multiply_reduce_fusion
  634.5 88.4 %scatter_custom_fusion = f32[2048,128]{1,0:T(8,128)S(1)} fusion(s32[16384]{0:T(1024)S(1)} %bitcast.51, bf16[16384,128]{1,0:T(8,128)(2,1)} %bitcast.19, f32[]{:T(128)} %constant.52.clone.1), kind=kCustom, calls=%fused_computation.20 | custom fusion | flops 4194304 | bytes 5242884 | tf_op jit(solution)/shard_map/scatter-add | solution.py:97
  723.8 12.8 %while.7 = (s32[]{:T(128)}, f32[256,128]{1,0:T(8,128)S(1)}, s32[8,2048]{1,0:T(8,128)S(1)}, bf16[8,2048,128]{2,1,0:T(8,128)(2,1)}, s32[]{:T(128)}, /*index=5*/s32[]{:T(128)}) while((s32[]{:T(128)}, f32[256,128]{1,0:T(8,128)S(1)}, s32[8,2048]{1,0:T(8,128)S(1)}, bf16[8,2048,128]{2,1,0:T(8,128)(2,1)}, s32[]{:T(128)}, ...), condition=%wide.region_1.2_spmd.clone, body=%wide.region_0.1_spmd.clone.sunk | while | flops 134807552 | bytes 811103 | solution.py:36
  737.9 34.6 %all-reduce.6.cloned.1.call-done = bf16[2048,128]{1,0:T(8,128)(2,1)} async-done(((bf16[2048,128]{1,0:T(8,128)(2,1)}), bf16[2048,128]{1,0:T(8,128)(2,1)}) %all-reduce.6.cloned.1.call-update) | async-done | bytes 524304 | tf_op jit(solution)/shard_map/psum | solution.py:102
  774.5 2.4 fusion.21
  (76 shorter events, 26.8 us)
Async XLA Ops:
  9.5 32.6 %all-to-all-start = ((s32[64,1,256]{2,1,0:T(1,128)}), s32[64,1,256]{2,1,0:T(1,128)S(1)}, u32[]{:S(2)}, u32[]{:S(2)}) async-start(s32[64,1,256]{2,1,0:T(1,128)} %all_to_all.16), calls=%async_computation | async-start | bytes 131072 | tf_op jit(solution)/shard_map/all_to_all | solution.py:82
  42.1 10.8 %copy-start = (f32[2048,128]{1,0:T(8,128)S(1)}, f32[2048,128]{1,0:T(8,128)}, u32[]{:S(2)}) copy-start(f32[2048,128]{1,0:T(8,128)} %param.15) | copy-start | bytes 3145732
  42.1 104.1 %all-to-all-start.2 = ((bf16[64,256,128]{2,1,0:T(8,128)(2,1)}), bf16[64,256,128]{2,1,0:T(8,128)(2,1)}, u32[]{:S(2)}, u32[]{:S(2)}) async-start(bf16[64,256,128]{2,1,0:T(8,128)(2,1)} %bitcast.50), calls=%async_computation.2 | async-start | bytes 8388608 | tf_op jit(solution)/shard_map/all_to_all | solution.py:96
  115.9 39.3 %copy-start.1 = (f32[4096,128]{1,0:T(8,128)S(1)}, f32[4096,128]{1,0:T(8,128)}, u32[]{:S(2)}) copy-start(f32[4096,128]{1,0:T(8,128)} %param.17) | copy-start | bytes 6291460
  146.2 577.6 %all-to-all-start.1 = ((bf16[64,256,128]{2,1,0:T(8,128)(2,1)}), bf16[64,256,128]{2,1,0:T(8,128)(2,1)}, u32[]{:S(2)}, u32[]{:S(2)}) async-start(bf16[64,256,128]{2,1,0:T(8,128)(2,1)} %select_convert_fusion), calls=%async_computation.1 | async-start | bytes 8388608 | tf_op jit(solution)/shard_map/all_to_all | solution.py:84
  154.6 206.9 %all-reduce.4.cloned.1.call-start = ((), (), s32[]{:S(2)}) async-start(), calls=%async_computation.3 | async-start | bytes 2097152 | tf_op jit(solution)/shard_map/psum | solution.py:14
  155.3 1.2 copy-start.4
  155.3 1.2 copy-start.7
  155.3 3.0 copy-start.5
  156.4 473.3 %all-reduce.8.cloned.1.call-start = ((), (), s32[]{:S(2)}) async-start(), calls=%async_computation.5 | async-start | bytes 4194304 | tf_op jit(solution)/shard_map/psum | solution.py:104
  171.5 601.0 %all-reduce.6.cloned.1.call-start = ((), (), s32[]{:S(2)}) async-start(), calls=%async_computation.4 | async-start | bytes 1048576 | tf_op jit(solution)/shard_map/psum | solution.py:102
  370.5 261.6 %copy-start.6 = (f32[4096]{0:T(1024)S(1)}, f32[4096]{0:T(1024)}, u32[]{:S(2)}) copy-start(f32[4096]{0:T(1024)} %param.18) | copy-start | bytes 49156
  629.7 3.0 copy-start.2
  723.8 12.8 %copy-start.3 = (bf16[2048,128]{1,0:T(8,128)(2,1)S(1)}, bf16[2048,128]{1,0:T(8,128)(2,1)}, u32[]{:S(2)}) copy-start(bf16[2048,128]{1,0:T(8,128)(2,1)} %gather_fusion.1) | copy-start | bytes 1572868
  736.6 37.3 %copy-start.8 = (f32[2048]{0:T(1024)S(1)}, f32[2048]{0:T(1024)}, u32[]{:S(2)}) copy-start(f32[2048]{0:T(1024)} %param.16) | copy-start | bytes 24580
Sparse Core Ops, SparseCore 0:
  159.4 202.0 all-reduce.3
  367.4 262.2 all-reduce.7
Sparse Core Ops, SparseCore 1:
  723.9 48.6 all-reduce.5
where the time goes:
time: 787 us; the launch traced here: 784 us
  waiting for transfers between devices  514 us (65%)
  other arithmetic  122 us (16%)
  local copies, waits for them, and re-layouts  67.8 us (9%)
  matrix products  34.6 us (4%)
  starting transfers between devices  29.5 us (4%)
  between operations  16.4 us (2%)
    psum x1, waiting for transfers between devices, shards(): hot_total = lax.psum(hot_dense, ('table', 'rep'))  259 us
    psum x1, waiting for transfers between devices, from_root(): return lax.psum(block, axis)  190 us
    scatter-add x1, other arithmetic, shards(): jax.ops.segment_sum(returned.reshape(-1, row_width).astype(jnp.float32),...  88.4 us
    gather x1, local copies, waits for them, and re-layouts, shards(): jnp.take(embedding_table, received_index, axis=0).astype(jnp.bfloat16)  55.4 us
    psum x1, waiting for transfers between devices, shards(): lax.psum(dense_grad.astype(jnp.bfloat16), 'rep').astype(jnp.float32)  34.6 us
    all_to_all x1, waiting for transfers between devices, shards(): lax.all_to_all(slot_grad, 'table', split_axis=0, concat_axis=0, tiled=True)  30.3 us
    dot_general x9, matrix products, one_block(): lax.dot_general(onehot, bag_grad, (((0,), (0,)), ((), ())), preferred_ele...  20.9 us
  transfers between devices with their start and end apart: 6, of which 4 were waited for; matrix products, arithmetic and copies ran while one was open for 28% of the time, Pallas kernels for 0%

commit v1 on v0

v1 whole, which is shorter than its diff:
```python
import functools

import jax
import jax.numpy as jnp
from jax import lax
from jax.experimental import pallas as pl
from jax.experimental.pallas import tpu as pltpu
from jax.sharding import PartitionSpec as P

learn_rate = 0.1
epsilon = 1e-08
LO = 256
GROUP = 4
bf16 = jnp.bfloat16
f32 = jnp.float32


def row_iota(n, m):
    return lax.broadcasted_iota(jnp.int32, (n, m), 0)


def onehot_rows(n, ids):
    return jnp.where(row_iota(n, ids.shape[1]) == ids, 1.0, 0.0).astype(bf16)


def code_parts(code):
    bag = jnp.where(code < 0, -1, code & (LO - 1))
    return code >> 16, (code >> 8) & (LO - 1), bag


def fold_table(table_ref, folded, high):
    width = table_ref.shape[1]
    for h in range(high):
        folded[h * width : (h + 1) * width, :] = table_ref[h * LO : (h + 1) * LO, :].astype(f32).T.astype(bf16)


def fetch(folded, code, high):
    width = folded.shape[0] // high
    hi, lo, bag = code_parts(code)
    every = jnp.dot(folded[...], onehot_rows(LO, lo), preferred_element_type=f32)
    picked = jnp.zeros((width, code.shape[1]), f32)
    for h in range(high):
        picked = jnp.where(hi == h, every[h * width : (h + 1) * width], picked)
    return picked.astype(bf16)


def pool(code, columns, bag_count):
    bag = code_parts(code)[2]
    return lax.dot_general(onehot_rows(bag_count, bag), columns, (((1,), (1,)), ((), ())), preferred_element_type=f32)


def scatter_terms(code, grad, high):
    hi, lo, bag = code_parts(code)
    spread = jnp.dot(grad, onehot_rows(grad.shape[1], bag), preferred_element_type=f32)
    parts = [jnp.where(hi == h, spread, 0.0).astype(bf16) for h in range(high)]
    return jnp.concatenate(parts, axis=0), onehot_rows(LO, lo)


def unfold(total, out_ref, high):
    width = out_ref.shape[1]
    for h in range(high):
        out_ref[h * LO : (h + 1) * LO, :] = total[h * width : (h + 1) * width, :].T.astype(out_ref.dtype)


def gather_kernel(high, code_ref, table_ref, out_ref, folded):
    @pl.when(pl.program_id(0) == 0)
    def _():
        fold_table(table_ref, folded, high)

    for k in range(GROUP):
        out_ref[k] = fetch(folded, code_ref[0, k : k + 1, :], high)


def gather_rows(codes, table):
    lists, slots = codes.shape
    rows, width = table.shape
    high = rows // LO
    return pl.pallas_call(
        functools.partial(gather_kernel, high),
        grid=(lists // GROUP,),
        in_specs=[
            pl.BlockSpec((1, GROUP, slots), lambda i: (i, 0, 0)),
            pl.BlockSpec((rows, width), lambda i: (0, 0)),
        ],
        out_specs=pl.BlockSpec((GROUP, width, slots), lambda i: (i, 0, 0)),
        out_shape=jax.ShapeDtypeStruct((lists, width, slots), bf16),
        scratch_shapes=[pltpu.VMEM((high * width, LO), bf16)],
        cost_estimate=pl.CostEstimate(flops=2 * lists * slots * rows * width, bytes_accessed=6 << 20, transcendentals=0),
        name="gather_rows",
    )(codes.reshape(lists // GROUP, GROUP, slots), table)


def pool_kernel(code_ref, columns_ref, start_ref, out_ref, total):
    step = pl.program_id(0)

    @pl.when(step == 0)
    def _():
        total[...] = start_ref[...]

    partial = pool(code_ref[0, 0:1, :], columns_ref[0], total.shape[0])
    for k in range(1, GROUP):
        partial = partial + pool(code_ref[0, k : k + 1, :], columns_ref[k], total.shape[0])
    total[...] += partial

    @pl.when(step == pl.num_programs(0) - 1)
    def _():
        out_ref[...] = total[...].astype(out_ref.dtype)


def pool_rows(codes, columns, start):
    lists, width, slots = columns.shape
    bags = start.shape[0]
    return pl.pallas_call(
        pool_kernel,
        grid=(lists // GROUP,),
        in_specs=[
            pl.BlockSpec((1, GROUP, slots), lambda i: (i, 0, 0)),
            pl.BlockSpec((GROUP, width, slots), lambda i: (i, 0, 0)),
            pl.BlockSpec((bags, width), lambda i: (0, 0)),
        ],
        out_specs=pl.BlockSpec((bags, width), lambda i: (0, 0)),
        out_shape=jax.ShapeDtypeStruct((bags, width), bf16),
        scratch_shapes=[pltpu.VMEM((bags, width), f32)],
        cost_estimate=pl.CostEstimate(flops=2 * lists * slots * bags * width, bytes_accessed=5 << 20, transcendentals=0),
        name="pool_rows",
    )(codes.reshape(lists // GROUP, GROUP, slots), columns, start)


def rowgrad_kernel(high, place_ref, code_ref, grad_ref, out_ref, total):
    step = pl.program_id(0)

    @pl.when(step == 0)
    def _():
        total[...] = jnp.zeros_like(total)

    terms, lows = [], []
    for k in range(GROUP):
        a, b = scatter_terms(code_ref[pl.ds(place_ref[step * GROUP + k], 1), :], grad_ref[k], high)
        terms.append(a)
        lows.append(b)
    total[...] += lax.dot_general(
        jnp.concatenate(terms, axis=1), jnp.concatenate(lows, axis=1), (((1,), (1,)), ((), ())), preferred_element_type=f32
    )

    @pl.when(step == pl.num_programs(0) - 1)
    def _():
        unfold(total, out_ref, high)


def row_gradients(place, codes, grads, rows):
    lists, slots = codes.shape
    _, width, bags = grads.shape
    high = rows // LO
    return pl.pallas_call(
        functools.partial(rowgrad_kernel, high),
        grid_spec=pltpu.PrefetchScalarGridSpec(
            num_scalar_prefetch=1,
            grid=(lists // GROUP,),
            in_specs=[
                pl.BlockSpec((lists, slots), lambda i, place: (0, 0)),
                pl.BlockSpec((GROUP, width, bags), lambda i, place: (i, 0, 0)),
            ],
            out_specs=pl.BlockSpec((rows, width), lambda i, place: (0, 0)),
            scratch_shapes=[pltpu.VMEM((high * width, LO), f32)],
        ),
        out_shape=jax.ShapeDtypeStruct((rows, width), bf16),
        cost_estimate=pl.CostEstimate(flops=2 * lists * slots * rows * width, bytes_accessed=5 << 20, transcendentals=0),
        name="row_gradients",
    )(place, codes, grads)


def hot_back_kernel(high, code_ref, grad_ref, out_ref, total):
    for k in range(code_ref.shape[0]):
        a, b = scatter_terms(code_ref[k : k + 1, :], grad_ref[...], high)
        part = lax.dot_general(a, b, (((1,), (1,)), ((), ())), preferred_element_type=f32)
        total[...] = part if k == 0 else total[...] + part
    unfold(total, out_ref, high)


def hot_gradients(codes, grad, rows):
    width = grad.shape[0]
    high = rows // LO
    return pl.pallas_call(
        functools.partial(hot_back_kernel, high),
        out_shape=jax.ShapeDtypeStruct((rows, width), bf16),
        scratch_shapes=[pltpu.VMEM((high * width, LO), f32)],
        cost_estimate=pl.CostEstimate(flops=2 * codes.size * rows * width, bytes_accessed=2 << 20, transcendentals=0),
        name="hot_gradients",
    )(codes, grad)


def hot_pool_kernel(high, code_ref, table_ref, out_ref, folded):
    fold_table(table_ref, folded, high)
    total = jnp.zeros(out_ref.shape, f32)
    for k in range(code_ref.shape[0]):
        code = code_ref[k : k + 1, :]
        total = total + pool(code, fetch(folded, code, high), out_ref.shape[0])
    out_ref[...] = total


def hot_pool(codes, table, bags):
    rows, width = table.shape
    high = rows // LO
    return pl.pallas_call(
        functools.partial(hot_pool_kernel, high),
        out_shape=jax.ShapeDtypeStruct((bags, width), f32),
        scratch_shapes=[pltpu.VMEM((high * width, LO), bf16)],
        cost_estimate=pl.CostEstimate(flops=2 * codes.size * rows * width, bytes_accessed=2 << 20, transcendentals=0),
        name="hot_pool",
    )(codes, table)


def exchange(x, axis):
    return lax.all_to_all(x, axis, split_axis=0, concat_axis=0, tiled=True)


def spread(x, axis, count):
    return exchange(jnp.broadcast_to(x[None], (count,) + x.shape), axis)


def adagrad_rows(weights, history, gradient):
    updated = history + jnp.mean(gradient * gradient, axis=1)
    return (weights - learn_rate * gradient / (jnp.sqrt(updated)[:, None] + epsilon), updated)


SIZE_Y, SIZE_Z, SIZE_C = 4, 8, 2


def shifted(dy, dz, dc):
    pairs = []
    for i in range(SIZE_Y * SIZE_Z * SIZE_C):
        y, z, c = i // (SIZE_Z * SIZE_C), i // SIZE_C % SIZE_Z, i % SIZE_C
        j = ((y + dy) % SIZE_Y * SIZE_Z + (z + dz) % SIZE_Z) * SIZE_C + (c + dc) % SIZE_C
        pairs.append((i, j))
    return pairs


def gather_grads(grad):
    along = jnp.stack([grad] + [lax.ppermute(grad, "table", shifted(0, s, 0)) for s in range(1, SIZE_Z)])
    plane = jnp.concatenate([along] + [lax.ppermute(along, "table", shifted(s, 0, 0)) for s in range(1, SIZE_Y)])
    return jnp.concatenate([plane, lax.ppermute(plane, "table", shifted(0, 0, 1))])


def sources():
    me = lax.axis_index("table")
    y, z, c = me // (SIZE_Z * SIZE_C), me // SIZE_C % SIZE_Z, me % SIZE_C
    k = jnp.arange(SIZE_Y * SIZE_Z * SIZE_C, dtype=jnp.int32)
    ky, kz, kc = k // SIZE_Z % SIZE_Y, k % SIZE_Z, k // (SIZE_Y * SIZE_Z)
    return ((y - ky) % SIZE_Y * SIZE_Z + (z - kz) % SIZE_Z) * SIZE_C + (c - kc) % SIZE_C


def shards(
    embedding_table,
    row_history,
    hot_table,
    hot_history,
    hot_owner,
    cold_index,
    cold_counts,
    cold_bags,
    hot_index,
    hot_bags,
    pooled_grad,
):
    peers = lax.axis_size("table")
    replicas = lax.axis_size("rep")
    rep = lax.axis_index("rep")
    hot_rows, width = hot_table.shape
    slots = cold_index.shape[2]
    bags = pooled_grad.shape[1]
    owner = hot_owner[0]

    live = jnp.arange(slots, dtype=jnp.int32)[None, :] < cold_counts[0][:, None]
    codes = jnp.where(live, cold_index[0] * LO + cold_bags[0], -1)
    hot_codes = (hot_index[0] * LO + hot_bags[0]).reshape(-1, LO)
    grad = pooled_grad[0].T

    asked = exchange(codes, "table")

    quarter = hot_rows // replicas
    piece = quarter // peers
    mine = lax.dynamic_slice_in_dim(hot_table, rep * quarter, quarter, 0).astype(bf16)
    pieces = exchange(mine.reshape(peers, piece, width), "table")
    own_piece = lax.dynamic_index_in_dim(pieces, owner, 0, keepdims=False)

    grads = gather_grads(grad)
    served = gather_rows(asked, embedding_table)
    pulled = exchange(served, "table")

    hot_quarter = spread(own_piece, "table", peers).reshape(quarter, width)
    hot_block = spread(hot_quarter, "rep", replicas).reshape(hot_rows, width)

    hot_part = hot_gradients(hot_codes, grad, hot_rows)
    by_replica = exchange(hot_part.reshape(replicas, quarter, width), "rep")
    quarter_sum = jnp.sum(by_replica.astype(f32), axis=0).astype(bf16)
    by_peer = exchange(quarter_sum.reshape(peers, piece, width), "table")
    piece_sum = jnp.sum(by_peer.astype(f32), axis=0)
    quarter_total = spread(piece_sum, "table", peers).reshape(quarter, width)
    hot_total = spread(quarter_total, "rep", replicas).reshape(hot_rows, width)

    dense = row_gradients(sources(), asked, grads, embedding_table.shape[0])
    ring = [[(i, (i + s) % replicas) for i in range(replicas)] for s in range(replicas)]
    total = dense.astype(f32)
    for s in range(1, replicas):
        total = total + lax.ppermute(dense, "rep", ring[s]).astype(f32)
    next_table, next_history = adagrad_rows(embedding_table, row_history, total)

    hot_updated, history_updated = adagrad_rows(hot_table, hot_history, hot_total)
    is_owner = lax.axis_index("table") == owner
    next_hot = jnp.where(is_owner, hot_updated, hot_table)
    next_squares = jnp.where(is_owner, history_updated, hot_history)

    hot_sum = hot_pool(hot_codes, hot_block, bags)
    pooled = pool_rows(codes, pulled, hot_sum)
    return (pooled[None], next_table, next_history, next_hot, next_squares)


def solution(mesh):
    in_specs = (
        P("table", None),
        P("table"),
        P("table", None),
        P("table"),
        P(),
        P("rep", "table", None),
        P("rep", "table"),
        P("rep", "table", None),
        P("rep", "table"),
        P("rep", "table"),
        P("rep", "table", None),
    )
    out_specs = (
        P("rep", "table", None),
        P("table", None),
        P("table"),
        P("table", None),
        P("table"),
    )
    return jax.shard_map(shards, mesh=mesh, in_specs=in_specs, out_specs=out_specs, check_vma=False)
```

time: 787 us -> 320 us (0.41)
  waiting for transfers between devices: 514 us -> 128 us
  other arithmetic: 122 us -> 12.9 us
  Pallas kernels: 0 us -> 55.8 us
  starting transfers between devices: 29.5 us -> 79.3 us
  local copies, waits for them, and re-layouts: 67.8 us -> 22.4 us
  matrix products: 34.6 us -> 0 us
  blocking collectives: 0 us -> 17.8 us
  between operations: 16.4 us -> 1.46 us
    psum x3 -> x0, waiting for transfers between devices: 484 us -> none  [the longest x1 259 us: shards(): hot_total = lax.psum(hot_dense, ('table', 'rep'))]
    scatter-add x2 -> x0, other arithmetic: 102 us -> none  [the longest x1 88.4 us: shards(): jax.ops.segment_sum(returned.reshape(-1, row_width).astype(jnp.float32),...]
    ppermute x0 -> x14, waiting for transfers between devices: none -> 71.6 us  [the longest x3 52.5 us: gather_grads(): lax.ppermute(along, 'table', shifted(s, 0, 0))]
    gather x2 -> x0, local copies, waits for them, and re-layouts: 64.5 us -> none  [the longest x1 55.4 us: shards(): jnp.take(embedding_table, received_index, axis=0).astype(jnp.bfloat16)]
    pallas_call x0 -> x5, Pallas kernels: none -> 55.8 us  [the longest x1 17.6 us: row_gradients(): pl.pallas_call(functools.partial(rowgrad_kernel, high), grid_spec=pltpu.P...]
    dot_general x18 -> x0, matrix products: 34.6 us -> none  [the longest x9 20.9 us: one_block(): lax.dot_general(onehot, bag_grad, (((0,), (0,)), ((), ())), preferred_ele...]
    all_to_all x3 -> x8, starting transfers between devices: 29.4 us -> 59.8 us  [exchange(): return lax.all_to_all(x, axis, split_axis=0, concat_axis=0, tiled=True)]
    all_to_all x3 -> x8, waiting for transfers between devices: 30.3 us -> 56.5 us  [exchange(): return lax.all_to_all(x, axis, split_axis=0, concat_axis=0, tiled=True)]
  transfers between devices with their start and end apart: 6 -> 22, of which waited for: 4 -> 11; matrix products, arithmetic and copies ran while one was open for 28% -> 10% of each run, Pallas kernels for 0% -> 14%
where the time goes in v1:
time: 320 us; the launch traced here: 318 us
  waiting for transfers between devices  128 us (40%)
  starting transfers between devices  79.3 us (25%)
  Pallas kernels  55.8 us (17%)
  local copies, waits for them, and re-layouts  22.4 us (7%)
  blocking collectives  17.8 us (6%)
  other arithmetic  12.9 us (4%)
    all_to_all x8, starting transfers between devices, exchange(): return lax.all_to_all(x, axis, split_axis=0, concat_axis=0, tiled=True)  59.8 us
    all_to_all x8, waiting for transfers between devices, exchange(): return lax.all_to_all(x, axis, split_axis=0, concat_axis=0, tiled=True)  56.5 us
    ppermute x3, waiting for transfers between devices, gather_grads(): lax.ppermute(along, 'table', shifted(s, 0, 0))  52.5 us
    all_to_all x1, blocking collectives, exchange(): return lax.all_to_all(x, axis, split_axis=0, concat_axis=0, tiled=True)  17.8 us
    pallas_call x1, Pallas kernels, row_gradients(): pl.pallas_call(functools.partial(rowgrad_kernel, high), grid_spec=pltpu.P...  17.6 us
    ppermute x3, waiting for transfers between devices, shards(): total = total + lax.ppermute(dense, 'rep', ring[s]).astype(f32)  15.9 us
    pallas_call x1, Pallas kernels, gather_rows(): pl.pallas_call(functools.partial(gather_kernel, high), grid=(lists // GRO...  14 us
    pallas_call x1, Pallas kernels, pool_rows(): pl.pallas_call(pool_kernel, grid=(lists // GROUP,), in_specs=[pl.BlockSpe...  11.3 us
  transfers between devices with their start and end apart: 22, of which 11 were waited for; matrix products, arithmetic and copies ran while one was open for 10% of the time, Pallas kernels for 14%

profile of v1, /device:TPU:128, one launch (start us, length us, event | category | flops | bytes accessed | tf_op | source)
XLA Modules:
  0.0 317.7 jit_solution(13875686864413807716)
XLA Ops:
  2.3 10.4 %all-to-all-start = ((s32[64,1,256]{2,1,0:T(1,128)}), s32[64,1,256]{2,1,0:T(1,128)S(1)}, u32[]{:S(2)}, u32[]{:S(2)}) async-start(s32[64,1,256]{2,1,0:T(1,128)} %get-tuple-element.7), calls=%async_computation | async-start | bytes 131072 | tf_op jit(solution)/shard_map/all_to_all | solution.py:214
  14.5 3.5 %all-to-all-done = s32[64,1,256]{2,1,0:T(1,128)S(1)} async-done(((s32[64,1,256]{2,1,0:T(1,128)}), s32[64,1,256]{2,1,0:T(1,128)S(1)}, u32[]{:S(2)}, u32[]{:S(2)}) %all-to-all-start) | async-done | bytes 65568 | tf_op jit(solution)/shard_map/all_to_all | solution.py:214
  18.0 9.0 %all-to-all-start.2 = ((bf16[64,16,128]{2,1,0:T(8,128)(2,1)}), bf16[64,16,128]{2,1,0:T(8,128)(2,1)S(1)}, u32[]{:S(2)}, u32[]{:S(2)}) async-start(bf16[64,16,128]{2,1,0:T(8,128)(2,1)} %bitcast.2), calls=%async_computation.2 | async-start | bytes 524288 | tf_op jit(solution)/shard_map/all_to_all | solution.py:214
  29.9 6.8 %hot_gradients.1 = bf16[4096,128]{1,0:T(8,128)(2,1)} custom-call(s32[8,256]{1,0:T(8,128)} %add.103.code_ref, bf16[128,256]{1,0:T(8,128)(2,1)} %bitcast.73), custom_call_target="tpu_custom_call" | custom-call | flops 2147483648 | bytes 2097152 | tf_op jit(solution)/shard_map/hot_gradients/pallas_call | solution.py:183
  36.8 4.3 %all-to-all-start.5 = ((bf16[4,1024,128]{2,1,0:T(8,128)(2,1)}), bf16[4,1024,128]{2,1,0:T(8,128)(2,1)S(1)}, u32[]{:S(2)}, u32[]{:S(2)}) async-start(bf16[4,1024,128]{2,1,0:T(8,128)(2,1)} %bitcast.72), calls=%async_computation.5 | async-start | bytes 2097152 | tf_op jit(solution)/shard_map/all_to_all | solution.py:214
  41.7 14.7 %all-to-all-done.5 = bf16[4,1024,128]{2,1,0:T(8,128)(2,1)S(1)} async-done(((bf16[4,1024,128]{2,1,0:T(8,128)(2,1)}), bf16[4,1024,128]{2,1,0:T(8,128)(2,1)S(1)}, u32[]{:S(2)}, u32[]{:S(2)}) %all-to-all-start.5) | async-done | bytes 1048608 | tf_op jit(solution)/shard_map/all_to_all | solution.py:214
  57.2 10.4 %all-to-all-start.3 = ((bf16[64,16,128]{2,1,0:T(8,128)(2,1)}), bf16[64,16,128]{2,1,0:T(8,128)(2,1)S(1)}, u32[]{:S(2)}, u32[]{:S(2)}) async-start(bf16[64,16,128]{2,1,0:T(8,128)(2,1)} %broadcast_in_dim.43), calls=%async_computation.3 | async-start | bytes 524288 | tf_op jit(solution)/shard_map/all_to_all | solution.py:214
  67.8 9.0 %all-to-all-done.3 = bf16[64,16,128]{2,1,0:T(8,128)(2,1)S(1)} async-done(((bf16[64,16,128]{2,1,0:T(8,128)(2,1)}), bf16[64,16,128]{2,1,0:T(8,128)(2,1)S(1)}, u32[]{:S(2)}, u32[]{:S(2)}) %all-to-all-start.3) | async-done | bytes 262176 | tf_op jit(solution)/shard_map/all_to_all | solution.py:214
  76.9 17.8 %all_to_all.48 = bf16[64,16,128]{2,1,0:T(8,128)(2,1)S(1)} all-to-all(bf16[64,16,128]{2,1,0:T(8,128)(2,1)S(1)} %bitcast.70), channel_id=1, replica_groups=mesh['table'=64,'rep'=4] {'table'}, dimensions={0} | all-to-all | bytes 524288 | tf_op jit(solution)/shard_map/all_to_all | solution.py:214
  95.8 3.6 %all-to-all-start.4 = ((bf16[4,1024,128]{2,1,0:T(8,128)(2,1)}), bf16[4,1024,128]{2,1,0:T(8,128)(2,1)S(1)}, u32[]{:S(2)}, u32[]{:S(2)}) async-start(bf16[4,1024,128]{2,1,0:T(8,128)(2,1)} %broadcast_in_dim.45), calls=%async_computation.4 | async-start | bytes 2097152 | tf_op jit(solution)/shard_map/all_to_all | solution.py:214
  99.5 15.5 %all-to-all-done.4 = bf16[4,1024,128]{2,1,0:T(8,128)(2,1)S(1)} async-done(((bf16[4,1024,128]{2,1,0:T(8,128)(2,1)}), bf16[4,1024,128]{2,1,0:T(8,128)(2,1)S(1)}, u32[]{:S(2)}, u32[]{:S(2)}) %all-to-all-start.4) | async-done | bytes 1048608 | tf_op jit(solution)/shard_map/all_to_all | solution.py:214
  116.2 8.5 %all-to-all-start.7 = ((f32[64,16,128]{2,1,0:T(8,128)}), f32[64,16,128]{2,1,0:T(8,128)S(1)}, u32[]{:S(2)}, u32[]{:S(2)}) async-start(f32[64,16,128]{2,1,0:T(8,128)} %broadcast_in_dim.47), calls=%async_computation.7 | async-start | bytes 1048576 | tf_op jit(solution)/shard_map/all_to_all | solution.py:214
  128.3 3.6 %collective-permute-start.3 = (bf16[128,256]{1,0:T(8,128)(2,1)S(1)}, bf16[128,256]{1,0:T(8,128)(2,1)S(1)}, u32[]{:S(2)}, u32[]{:S(2)}) collective-permute-start(bf16[128,256]{1,0:T(8,128)(2,1)S(1)} %bitcast.77), channel_id=1, source_target_pairs={{0,32},{4,36},{8,40},{12,44},{16,48},{20,52},{24,56},{28,60},{32,0... | collective-permute-start | bytes 196616 | tf_op jit(solution)/shard_map/ppermute | solution.py:239
  134.2 9.4 %all-to-all-done.7 = f32[64,16,128]{2,1,0:T(8,128)S(1)} async-done(((f32[64,16,128]{2,1,0:T(8,128)}), f32[64,16,128]{2,1,0:T(8,128)S(1)}, u32[]{:S(2)}, u32[]{:S(2)}) %all-to-all-start.7) | async-done | bytes 524320 | tf_op jit(solution)/shard_map/all_to_all | solution.py:214
  145.1 3.6 %all-to-all-start.8 = ((f32[4,1024,128]{2,1,0:T(8,128)}), f32[4,1024,128]{2,1,0:T(8,128)S(1)}, u32[]{:S(2)}, u32[]{:S(2)}) async-start(f32[4,1024,128]{2,1,0:T(8,128)} %broadcast_in_dim.49), calls=%async_computation.8 | async-start | bytes 4194304 | tf_op jit(solution)/shard_map/all_to_all | solution.py:214
  153.2 14.0 %gather_rows.1 = bf16[64,128,256]{2,1,0:T(8,128)(2,1)} custom-call(s32[16,4,256]{2,1,0:T(4,128)} %reshape.125.code_ref, f32[2048,128]{1,0:T(8,128)} %table_ref.1), custom_call_target="tpu_custom_call" | custom-call | flops 8589934592 | bytes 6291456 | tf_op jit(solution)/shard_map/gather_rows/pallas_call | solution.py:78
  167.2 4.4 %all-to-all-done.8 = f32[4,1024,128]{2,1,0:T(8,128)S(1)} async-done(((f32[4,1024,128]{2,1,0:T(8,128)}), f32[4,1024,128]{2,1,0:T(8,128)S(1)}, u32[]{:S(2)}, u32[]{:S(2)}) %all-to-all-start.8) | async-done | bytes 2097184 | tf_op jit(solution)/shard_map/all_to_all | solution.py:214
  171.6 9.9 %all-to-all-start.1 = ((bf16[64,128,256]{2,1,0:T(8,128)(2,1)}), bf16[64,128,256]{2,1,0:T(8,128)(2,1)}, u32[]{:S(2)}, u32[]{:S(2)}) async-start(bf16[64,128,256]{2,1,0:T(8,128)(2,1)} %gather_rows.1), calls=%async_computation.1 | async-start | bytes 8388608 | tf_op jit(solution)/shard_map/all_to_all | solution.py:214
  189.9 28.2 %collective-permute-done.7 = bf16[8,128,256]{2,1,0:T(8,128)(2,1)S(1)} collective-permute-done((bf16[8,128,256]{2,1,0:T(8,128)(2,1)S(1)}, bf16[8,128,256]{2,1,0:T(8,128)(2,1)S(1)}, u32[]{:S(2)}, u32[]{:S(2)}) %collective-permute-start.7) | collective-permute-done | bytes 524320 | tf_op jit(solution)/shard_map/ppermute | solution.py:240
  219.2 24.3 %collective-permute-done.8 = bf16[8,128,256]{2,1,0:T(8,128)(2,1)S(1)} collective-permute-done((bf16[8,128,256]{2,1,0:T(8,128)(2,1)S(1)}, bf16[8,128,256]{2,1,0:T(8,128)(2,1)S(1)}, u32[]{:S(2)}, u32[]{:S(2)}) %collective-permute-start.8) | collective-permute-done | bytes 524320 | tf_op jit(solution)/shard_map/ppermute | solution.py:240
  253.3 17.6 %row_gradients.1 = bf16[2048,128]{1,0:T(8,128)(2,1)} custom-call(s32[64]{0:T(128)} %fusion.4.place_ref, s32[64,256]{1,0:T(8,128)} %bitcast.82, bf16[64,128,256]{2,1,0:T(8,128)(2,1)} %constant_dynamic-update-slice_fusion.19.grad_ref), custom_call_target="tpu_custom_call" | custom-call | flops 8589934592 | bytes 5242880 | tf_op jit(solution)/shard_map/row_gradients/pallas_call | solution.py:154
  276.3 6.1 %hot_pool.1.start_ref = f32[256,128]{1,0:T(8,128)} custom-call(s32[8,256]{1,0:T(8,128)} %add.103.code_ref, bf16[4096,128]{1,0:T(8,128)(2,1)} %bitcast.71), custom_call_target="tpu_custom_call" | custom-call | flops 2147483648 | bytes 2097152 | tf_op jit(solution)/shard_map/hot_pool/pallas_call | solution.py:204
  282.4 15.1 %collective-permute-done.11 = bf16[2048,128]{1,0:T(8,128)(2,1)S(1)} collective-permute-done((bf16[2048,128]{1,0:T(8,128)(2,1)}, bf16[2048,128]{1,0:T(8,128)(2,1)S(1)}, u32[]{:S(2)}, u32[]{:S(2)}) %collective-permute-start.11) | collective-permute-done | bytes 524320 | tf_op jit(solution)/shard_map/ppermute | solution.py:305
  306.5 11.3 %pool_rows.1 = bf16[256,128]{1,0:T(8,128)(2,1)} custom-call(s32[16,4,256]{2,1,0:T(4,128)} %fusion.code_ref, bf16[64,128,256]{2,1,0:T(8,128)(2,1)} %all-to-all-done.1.columns_ref, f32[256,128]{1,0:T(8,128)} %hot_pool.1.start_ref), custom_call_target="tpu_custom_call" | custom-call | flops 1073741824 | bytes 5242880 | tf_op jit(solution)/shard_map/pool_rows/pallas_call | solution.py:113
  (83 shorter events, 55.2 us)
Async XLA Ops:
  2.3 15.7 %all-to-all-start = ((s32[64,1,256]{2,1,0:T(1,128)}), s32[64,1,256]{2,1,0:T(1,128)S(1)}, u32[]{:S(2)}, u32[]{:S(2)}) async-start(s32[64,1,256]{2,1,0:T(1,128)} %get-tuple-element.7), calls=%async_computation | async-start | bytes 131072 | tf_op jit(solution)/shard_map/all_to_all | solution.py:214
  18.0 18.7 %all-to-all-start.2 = ((bf16[64,16,128]{2,1,0:T(8,128)(2,1)}), bf16[64,16,128]{2,1,0:T(8,128)(2,1)S(1)}, u32[]{:S(2)}, u32[]{:S(2)}) async-start(bf16[64,16,128]{2,1,0:T(8,128)(2,1)} %bitcast.2), calls=%async_computation.2 | async-start | bytes 524288 | tf_op jit(solution)/shard_map/all_to_all | solution.py:214
  36.8 19.7 %all-to-all-start.5 = ((bf16[4,1024,128]{2,1,0:T(8,128)(2,1)}), bf16[4,1024,128]{2,1,0:T(8,128)(2,1)S(1)}, u32[]{:S(2)}, u32[]{:S(2)}) async-start(bf16[4,1024,128]{2,1,0:T(8,128)(2,1)} %bitcast.72), calls=%async_computation.5 | async-start | bytes 2097152 | tf_op jit(solution)/shard_map/all_to_all | solution.py:214
  57.2 19.7 %all-to-all-start.3 = ((bf16[64,16,128]{2,1,0:T(8,128)(2,1)}), bf16[64,16,128]{2,1,0:T(8,128)(2,1)S(1)}, u32[]{:S(2)}, u32[]{:S(2)}) async-start(bf16[64,16,128]{2,1,0:T(8,128)(2,1)} %broadcast_in_dim.43), calls=%async_computation.3 | async-start | bytes 524288 | tf_op jit(solution)/shard_map/all_to_all | solution.py:214
  95.8 29.0 %copy-start.4 = (bf16[1,256,128]{1,2,0:T(8,128)(2,1)S(1)}, bf16[1,256,128]{1,2,0:T(8,128)(2,1)}, u32[]{:S(2)}) copy-start(bf16[1,256,128]{1,2,0:T(8,128)(2,1)} %copy.23) | copy-start | bytes 196612
  95.8 19.3 %all-to-all-start.4 = ((bf16[4,1024,128]{2,1,0:T(8,128)(2,1)}), bf16[4,1024,128]{2,1,0:T(8,128)(2,1)S(1)}, u32[]{:S(2)}, u32[]{:S(2)}) async-start(bf16[4,1024,128]{2,1,0:T(8,128)(2,1)} %broadcast_in_dim.45), calls=%async_computation.4 | async-start | bytes 2097152 | tf_op jit(solution)/shard_map/all_to_all | solution.py:214
  116.2 27.4 %all-to-all-start.7 = ((f32[64,16,128]{2,1,0:T(8,128)}), f32[64,16,128]{2,1,0:T(8,128)S(1)}, u32[]{:S(2)}, u32[]{:S(2)}) async-start(f32[64,16,128]{2,1,0:T(8,128)} %broadcast_in_dim.47), calls=%async_computation.7 | async-start | bytes 1048576 | tf_op jit(solution)/shard_map/all_to_all | solution.py:214
  124.7 24.7 %collective-permute-start = (bf16[128,256]{1,0:T(8,128)(2,1)S(1)}, bf16[128,256]{1,0:T(8,128)(2,1)S(1)}, u32[]{:S(2)}, u32[]{:S(2)}) collective-permute-start(bf16[128,256]{1,0:T(8,128)(2,1)S(1)} %bitcast.74), channel_id=1, source_target_pairs={{0,8},{4,12},{8,16},{12,20},{16,24},{20,28},{24,32},{28,36},{32,40... | collective-permute-start | bytes 196616 | tf_op jit(solution)/shard_map/ppermute | solution.py:239
  125.4 25.7 %collective-permute-start.1 = (bf16[128,256]{1,0:T(8,128)(2,1)S(1)}, bf16[128,256]{1,0:T(8,128)(2,1)S(1)}, u32[]{:S(2)}, u32[]{:S(2)}) collective-permute-start(bf16[128,256]{1,0:T(8,128)(2,1)S(1)} %bitcast.75), channel_id=1, source_target_pairs={{0,16},{4,20},{8,24},{12,28},{16,32},{20,36},{24,40},{28,44},{32,4... | collective-permute-start | bytes 196616 | tf_op jit(solution)/shard_map/ppermute | solution.py:239
  126.0 25.8 %collective-permute-start.2 = (bf16[128,256]{1,0:T(8,128)(2,1)S(1)}, bf16[128,256]{1,0:T(8,128)(2,1)S(1)}, u32[]{:S(2)}, u32[]{:S(2)}) collective-permute-start(bf16[128,256]{1,0:T(8,128)(2,1)S(1)} %bitcast.76), channel_id=1, source_target_pairs={{0,24},{4,28},{8,32},{12,36},{16,40},{20,44},{24,48},{28,52},{32,5... | collective-permute-start | bytes 196616 | tf_op jit(solution)/shard_map/ppermute | solution.py:239
  128.3 53.2 %collective-permute-start.3 = (bf16[128,256]{1,0:T(8,128)(2,1)S(1)}, bf16[128,256]{1,0:T(8,128)(2,1)S(1)}, u32[]{:S(2)}, u32[]{:S(2)}) collective-permute-start(bf16[128,256]{1,0:T(8,128)(2,1)S(1)} %bitcast.77), channel_id=1, source_target_pairs={{0,32},{4,36},{8,40},{12,44},{16,48},{20,52},{24,56},{28,60},{32,0... | collective-permute-start | bytes 196616 | tf_op jit(solution)/shard_map/ppermute | solution.py:239
  131.9 50.3 %collective-permute-start.4 = (bf16[128,256]{1,0:T(8,128)(2,1)S(1)}, bf16[128,256]{1,0:T(8,128)(2,1)S(1)}, u32[]{:S(2)}, u32[]{:S(2)}) collective-permute-start(bf16[128,256]{1,0:T(8,128)(2,1)S(1)} %bitcast.78), channel_id=1, source_target_pairs={{0,40},{4,44},{8,48},{12,52},{16,56},{20,60},{24,0},{28,4},{32,8},... | collective-permute-start | bytes 196616 | tf_op jit(solution)/shard_map/ppermute | solution.py:239
  145.1 26.5 %all-to-all-start.8 = ((f32[4,1024,128]{2,1,0:T(8,128)}), f32[4,1024,128]{2,1,0:T(8,128)S(1)}, u32[]{:S(2)}, u32[]{:S(2)}) async-start(f32[4,1024,128]{2,1,0:T(8,128)} %broadcast_in_dim.49), calls=%async_computation.8 | async-start | bytes 4194304 | tf_op jit(solution)/shard_map/all_to_all | solution.py:214
  149.4 33.4 %collective-permute-start.5 = (bf16[128,256]{1,0:T(8,128)(2,1)S(1)}, bf16[128,256]{1,0:T(8,128)(2,1)S(1)}, u32[]{:S(2)}, u32[]{:S(2)}) collective-permute-start(bf16[128,256]{1,0:T(8,128)(2,1)S(1)} %bitcast.79), channel_id=1, source_target_pairs={{0,48},{4,52},{8,56},{12,60},{16,0},{20,4},{24,8},{28,12},{32,16},... | collective-permute-start | bytes 196616 | tf_op jit(solution)/shard_map/ppermute | solution.py:239
  151.1 32.4 %collective-permute-start.6 = (bf16[128,256]{1,0:T(8,128)(2,1)S(1)}, bf16[128,256]{1,0:T(8,128)(2,1)S(1)}, u32[]{:S(2)}, u32[]{:S(2)}) collective-permute-start(bf16[128,256]{1,0:T(8,128)(2,1)S(1)} %bitcast.80), channel_id=1, source_target_pairs={{0,56},{4,60},{8,0},{12,4},{16,8},{20,12},{24,16},{28,20},{32,24},... | collective-permute-start | bytes 196616 | tf_op jit(solution)/shard_map/ppermute | solution.py:239
  171.6 134.9 %all-to-all-start.1 = ((bf16[64,128,256]{2,1,0:T(8,128)(2,1)}), bf16[64,128,256]{2,1,0:T(8,128)(2,1)}, u32[]{:S(2)}, u32[]{:S(2)}) async-start(bf16[64,128,256]{2,1,0:T(8,128)(2,1)} %gather_rows.1), calls=%async_computation.1 | async-start | bytes 8388608 | tf_op jit(solution)/shard_map/all_to_all | solution.py:214
  184.2 33.9 %collective-permute-start.7 = (bf16[8,128,256]{2,1,0:T(8,128)(2,1)S(1)}, bf16[8,128,256]{2,1,0:T(8,128)(2,1)S(1)}, u32[]{:S(2)}, u32[]{:S(2)}) collective-permute-start(bf16[8,128,256]{2,1,0:T(8,128)(2,1)S(1)} %get-tuple-element.19), channel_id=1, source_target_pairs={{0,64},{4,68},{8,72},{12,76},{16,80},{20,84},{24,88},{28,92},{32,9... | collective-permute-start | bytes 1572872 | tf_op jit(solution)/shard_map/ppermute | solution.py:240
  185.7 57.8 %collective-permute-start.8 = (bf16[8,128,256]{2,1,0:T(8,128)(2,1)S(1)}, bf16[8,128,256]{2,1,0:T(8,128)(2,1)S(1)}, u32[]{:S(2)}, u32[]{:S(2)}) collective-permute-start(bf16[8,128,256]{2,1,0:T(8,128)(2,1)S(1)} %get-tuple-element.19), channel_id=1, source_target_pairs={{0,128},{4,132},{8,136},{12,140},{16,144},{20,148},{24,152},{28,15... | collective-permute-start | bytes 1572872 | tf_op jit(solution)/shard_map/ppermute | solution.py:240
  188.6 56.0 %collective-permute-start.9 = (bf16[8,128,256]{2,1,0:T(8,128)(2,1)S(1)}, bf16[8,128,256]{2,1,0:T(8,128)(2,1)S(1)}, u32[]{:S(2)}, u32[]{:S(2)}) collective-permute-start(bf16[8,128,256]{2,1,0:T(8,128)(2,1)S(1)} %get-tuple-element.19), channel_id=1, source_target_pairs={{0,192},{4,196},{8,200},{12,204},{16,208},{20,212},{24,216},{28,22... | collective-permute-start | bytes 1572872 | tf_op jit(solution)/shard_map/ppermute | solution.py:240
  245.6 4.5 %collective-permute-start.10 = (bf16[32,128,256]{2,1,0:T(8,128)(2,1)}, bf16[32,128,256]{2,1,0:T(8,128)(2,1)}, u32[]{:S(2)}, u32[]{:S(2)}) collective-permute-start(bf16[32,128,256]{2,1,0:T(8,128)(2,1)} %get-tuple-element.11), channel_id=1, source_target_pairs={{0,4},{4,0},{8,12},{12,8},{16,20},{20,16},{24,28},{28,24},{32,36},... | collective-permute-start | bytes 6291464 | tf_op jit(solution)/shard_map/ppermute | solution.py:241
  270.9 26.6 %collective-permute-start.11 = (bf16[2048,128]{1,0:T(8,128)(2,1)}, bf16[2048,128]{1,0:T(8,128)(2,1)S(1)}, u32[]{:S(2)}, u32[]{:S(2)}) collective-permute-start(bf16[2048,128]{1,0:T(8,128)(2,1)} %row_gradients.1), channel_id=1, source_target_pairs={{0,1},{1,2},{2,3},{3,0},{4,5},{5,6},{6,7},{7,4},{8,9},{9,10},{10,1... | collective-permute-start | bytes 1572872 | tf_op jit(solution)/shard_map/ppermute | solution.py:305
  271.4 26.1 %collective-permute-start.12 = (bf16[2048,128]{1,0:T(8,128)(2,1)}, bf16[2048,128]{1,0:T(8,128)(2,1)}, u32[]{:S(2)}, u32[]{:S(2)}) collective-permute-start(bf16[2048,128]{1,0:T(8,128)(2,1)} %row_gradients.1), channel_id=1, source_target_pairs={{0,2},{1,3},{2,0},{3,1},{4,6},{5,7},{6,4},{7,5},{8,10},{9,11},{10,... | collective-permute-start | bytes 1572872 | tf_op jit(solution)/shard_map/ppermute | solution.py:305
  273.5 24.7 %collective-permute-start.13 = (bf16[2048,128]{1,0:T(8,128)(2,1)}, bf16[2048,128]{1,0:T(8,128)(2,1)}, u32[]{:S(2)}, u32[]{:S(2)}) collective-permute-start(bf16[2048,128]{1,0:T(8,128)(2,1)} %row_gradients.1), channel_id=1, source_target_pairs={{0,3},{1,0},{2,1},{3,2},{4,7},{5,4},{6,5},{7,6},{8,11},{9,8},{10,9... | collective-permute-start | bytes 1572872 | tf_op jit(solution)/shard_map/ppermute | solution.py:305
  276.3 21.9 %copy-start.1 = (bf16[2048,128]{1,0:T(8,128)(2,1)S(1)}, bf16[2048,128]{1,0:T(8,128)(2,1)}, u32[]{:S(2)}) copy-start(bf16[2048,128]{1,0:T(8,128)(2,1)} %row_gradients.1) | copy-start | bytes 1572868
  (6 other events, 60.5 us)
